TPU v7x, 32 devices: a whole 2x2x4 slice. The times are simulated.
32 devices in a mesh: row: 8 (over y, x, core), col: 4 (over z).
Axes of the slice: x: 2, y: 2, z: 4, core: 2. Of those that a mesh axis runs over, the one named last changes fastest.
Arguments:
- mode_block: float32 [32768, 256], P(('row', 'col')), may hold values from -80 to 80
- k_blocks: float32 [256, 3, 128, 128], P(('row', 'col')), may hold values from -1 to 9
- block_cols: int32 [256, 3], P(('row', 'col')), may hold values from 0 to 255, as said below
- panel_node: int32 [4096], replicated, may hold values from 0 to 32767, as said below
- added_mass: bfloat16 [4096, 4096], P('row', 'col'), may hold values from -0.125 to 0.125
- low_edge: int32 [256], replicated, may hold values from 4 to 8
- high_edge: int32 [256], replicated, may hold values from 40 to 56
Outputs:
- filtered: float32 [32768, 256], P(('row', 'col'))
Inputs may be any that keep to these rules, and one draw needn't show every extreme that they name: `panel_node`: distinct shell rows. Cut the panels into 32 aligned blocks of 128; in each block at most 8 panels lie on the 1024 rows of one shell device (rows d * 1024 to (d + 1) * 1024 - 1), exactly 8 for some device, and the panels of a block on one device are consecutive. `block_cols`: row i holds i first, then two different block rows among i - 2 to i + 2 other than i.
All inputs are finite; a program needn't handle non-finite values.
Results may differ from a plain program's by a relative error of at most 0.0015.
Values may be sent and summed in bfloat16 or wider, within the bound.
A program may use at most 64 MiB of HBM per device.

v0:
```python
import jax
import jax.numpy as jnp
from jax import lax
from jax.sharding import PartitionSpec as P

DEGREE = 3
OUTER = 2


def with_halo(block, sides, width):
    for axis, dim in sides:
        count = lax.axis_size(axis)
        forward = [(i, i + 1) for i in range(count - 1)]
        backward = [(target, source) for source, target in forward]
        low = lax.ppermute(
            lax.slice_in_dim(block, block.shape[dim] - width, None, axis=dim), axis, forward
        )
        high = lax.ppermute(lax.slice_in_dim(block, 0, width, axis=dim), axis, backward)
        block = jnp.concatenate([low, block, high], axis=dim)
    return block


def body(mode_block, k_blocks, block_cols, panel_node, added_mass, low_edge, high_edge):
    n_row = lax.axis_size("row")
    n_col = lax.axis_size("col")
    devices = n_row * n_col
    my_row = lax.axis_index("row")
    my_col = lax.axis_index("col")
    linear = my_row * n_col + my_col
    rows_dev = mode_block.shape[0]
    mode_width = mode_block.shape[1]
    block_size = k_blocks.shape[2]
    blocks_dev = rows_dev // block_size
    panel_count = panel_node.shape[0]
    per_block = panel_count // devices
    slot_count = 2 * ((per_block + devices - 1) // devices)
    flat_total = devices * slot_count
    panel_rows = panel_node.reshape(devices, per_block)
    source = panel_rows // rows_dev
    within = jnp.arange(per_block)
    earlier = within[None, :] < within[:, None]
    same_source = source[:, :, None] == source[:, None, :]
    slot_rank = jnp.sum((same_source & earlier[None, :, :]).astype(jnp.int32), axis=2)
    block_ids = jnp.arange(devices)[:, None]
    target = block_ids % n_row * n_col + block_ids // n_row
    owned = source == linear
    local_row = panel_rows - linear * rows_dev
    send_flat = jnp.where(owned, target * slot_count + slot_rank, flat_total)
    send_index = jnp.full((flat_total,), rows_dev, dtype=jnp.int32)
    send_index = send_index.at[send_flat.reshape(-1)].set(local_row.reshape(-1), mode="drop")
    return_rows = jnp.where(owned, local_row, rows_dev)
    return_index = jnp.full((rows_dev,), flat_total, dtype=jnp.int32)
    return_index = return_index.at[return_rows.reshape(-1)].set(
        (block_ids * slot_count + slot_rank).reshape(-1), mode="drop"
    )
    in_block = my_col * n_row + my_row
    in_source = lax.dynamic_index_in_dim(source, in_block, 0, keepdims=False)
    in_slot = lax.dynamic_index_in_dim(slot_rank, in_block, 0, keepdims=False)
    in_flat = in_source * slot_count + in_slot
    out_source = lax.dynamic_index_in_dim(source, linear, 0, keepdims=False)
    out_slot = lax.dynamic_index_in_dim(slot_rank, linear, 0, keepdims=False)
    out_index = jnp.full((flat_total,), per_block, dtype=jnp.int32)
    out_index = out_index.at[out_source * slot_count + out_slot].set(within)
    row_source = lax.dynamic_slice_in_dim(source, my_row * n_col, n_col, 0)
    row_slot = lax.dynamic_slice_in_dim(slot_rank, my_row * n_col, n_col, 0)
    row_flat = (
        row_source * (n_col * slot_count) + jnp.arange(n_col)[:, None] * slot_count + row_slot
    )
    part_index = jnp.full((devices * n_col * slot_count,), n_col * per_block, dtype=jnp.int32)
    part_index = part_index.at[row_flat.reshape(-1)].set(jnp.arange(n_col * per_block))
    local_cols = block_cols - (linear * blocks_dev - 2)
    zero_bf = jnp.zeros((1, mode_width), jnp.bfloat16)
    zero_row = jnp.zeros((1, mode_width), jnp.float32)

    def stiffness(vectors):
        padded = with_halo(vectors, ((("row", "col"), 0),), 2 * block_size)
        pieces = padded.reshape(blocks_dev + 4, block_size, mode_width)
        chosen = pieces[local_cols]
        product = jnp.einsum("rkij,rkjn->rin", k_blocks, chosen, precision=lax.Precision.HIGHEST)
        return product.reshape(rows_dev, mode_width)

    def accumulate(arrived_piece):
        return jnp.dot(added_mass, arrived_piece, preferred_element_type=jnp.float32)

    def fluid_loads(vectors):
        rounded = jnp.concatenate([vectors.astype(jnp.bfloat16), zero_bf], axis=0)
        outgoing = rounded[send_index]
        arrived = lax.all_to_all(
            outgoing.reshape(devices, slot_count, mode_width),
            ("row", "col"),
            split_axis=0,
            concat_axis=0,
            tiled=True,
        )
        arrived = arrived.reshape(flat_total, mode_width)
        wetted = arrived[in_flat]
        partial_value = accumulate(lax.all_gather(wetted, "row", axis=0, tiled=True))
        pressure = lax.psum_scatter(partial_value, "col", scatter_dimension=0, tiled=True)
        padded_press = jnp.concatenate([pressure, zero_row], axis=0)
        sending = padded_press[out_index].reshape(devices, slot_count, mode_width)
        summed = lax.all_to_all(
            sending, ("row", "col"), split_axis=0, concat_axis=0, tiled=True
        ).reshape(flat_total, mode_width)
        padded_sum = jnp.concatenate([summed, zero_row], axis=0)
        return padded_sum[return_index]

    def operate(vectors):
        return stiffness(vectors) + fluid_loads(vectors)

    lower = low_edge.astype(jnp.float32) * 0.25
    upper = high_edge.astype(jnp.float32) * 0.25
    centre = 0.5 * (upper + lower)
    radius = 0.5 * (upper - lower)
    total_rows = rows_dev * devices
    current = mode_block
    for outer_no in range(OUTER):
        previous = current
        current = (operate(current) - centre * current) / radius
        for degree_no in range(DEGREE - 1):
            following = 2.0 * (operate(current) - centre * current) / radius - previous
            previous = current
            current = following
        squares = lax.psum(jnp.sum(current * current, axis=0), ("row", "col"))
        current = current / jnp.sqrt(squares / total_rows + 1e-06)
    return current


def solution(mesh):
    placed = (
        P(("row", "col"), None),
        P(("row", "col"), None, None, None),
        P(("row", "col"), None),
        P(),
        P("row", "col"),
        P(),
        P(),
    )
    return jax.shard_map(
        body, mesh=mesh, in_specs=placed, out_specs=P(("row", "col"), None), check_vma=False
    )
```

profile of v0, /device:TPU:0, one launch (start us, length us, event | category | flops | bytes accessed | tf_op | source)
XLA Modules:
  0.0 587.2 jit_solution(11731140511086322295)
XLA Ops:
  9.5 15.5 %scatter_custom_fusion = s32[256]{0:T(256)S(1)} fusion(s32[4096]{0:T(1024)S(1)} %get-tuple-element.35, s32[4096]{0:T(1024)S(1)} %get-tuple-element.20, s32[]{:T(128)} %constant.94.clone.1), kind=kCustom, calls=%fused_computation.139 | custom fusion | bytes 1028 | tf_op jit(solution)/shard_map/scatter | solution.py:50
  28.2 7.3 %all-to-all-start = ((bf16[32,8,256]{2,1,0:T(8,128)(2,1)}), bf16[32,8,256]{2,1,0:T(8,128)(2,1)S(1)}, u32[]{:S(2)}, u32[]{:S(2)}) async-start(bf16[32,8,256]{2,1,0:T(8,128)(2,1)} %bitcast.8), calls=%async_computation | async-start | bytes 262144 | tf_op jit(solution)/shard_map/all_to_all | solution.py:88
  37.4 3.7 collective-permute-start
  44.8 13.9 %all-gather = bf16[1024,256]{1,0:T(8,128)(2,1)S(1)} all-gather(bf16[128,256]{1,0:T(8,128)(2,1)S(1)} %gather_fusion.2), channel_id=2, replica_groups=mesh['row'=8,'col'=4] {'row'}, dimensions={0}, use_global_device_ids=true | all-gather | bytes 589824 | tf_op jit(solution)/shard_map/all_gather | solution.py:97
  60.3 15.5 %scatter_custom_fusion.2 = s32[1024]{0:T(1024)S(1)} fusion(s32[4096]{0:T(1024)S(1)} %get-tuple-element.19, s32[4096]{0:T(1024)S(1)} %add_bitcast_fusion, s32[]{:T(128)} %constant.101.clone.1), kind=kCustom, calls=%fused_computation.110 | custom fusion | bytes 4100 | tf_op jit(solution)/shard_map/scatter | solution.py:53
  75.8 4.1 reduce-scatter.7.cloned.1.call-done
  82.6 2.9 all-to-all-start.1
  85.5 2.6 pad_maximum_fusion
  88.1 3.8 gather_fusion
  91.9 5.1 fusion.59
  97.1 4.7 gather_fusion.4
  101.8 3.0 fusion.51
  106.0 14.0 %all_to_all.60 = bf16[32,8,256]{2,1,0:T(8,128)(2,1)S(1)} all-to-all(bf16[32,8,256]{2,1,0:T(8,128)(2,1)S(1)} %bitcast.215), channel_id=1, replica_groups=mesh['row'=8,'col'=4] {'row','col'}, dimensions={0} | all-to-all | bytes 262144 | tf_op jit(solution)/shard_map/all_to_all | solution.py:88
  120.8 9.6 %all-gather.1 = bf16[1024,256]{1,0:T(8,128)(2,1)S(1)} all-gather(bf16[128,256]{1,0:T(8,128)(2,1)S(1)} %gather_fusion.7), channel_id=3, replica_groups=mesh['row'=8,'col'=4] {'row'}, dimensions={0}, use_global_device_ids=true | all-gather | bytes 589824 | tf_op jit(solution)/shard_map/all_gather | solution.py:97
  131.7 1.9 fusion.57
  136.7 20.1 %reduce-scatter.9.cloned.1.call-done = f32[128,256]{0,1:T(8,128)} async-done(((f32[512,256]{0,1:T(8,128)}), f32[128,256]{0,1:T(8,128)}) %reduce-scatter.9.cloned.1.call-update) | async-done | bytes 131088 | tf_op jit(solution)/shard_map/reduce_scatter | solution.py:98
  159.5 4.7 all-to-all-start.3
  164.2 2.6 pad_maximum_fusion.1
  166.8 3.8 gather_fusion.5
  170.6 5.1 fusion.60
  175.8 4.7 gather_fusion.9
  180.5 3.4 fusion.49
  185.1 14.0 %all_to_all.61 = bf16[32,8,256]{2,1,0:T(8,128)(2,1)S(1)} all-to-all(bf16[32,8,256]{2,1,0:T(8,128)(2,1)S(1)} %bitcast.216), channel_id=1, replica_groups=mesh['row'=8,'col'=4] {'row','col'}, dimensions={0} | all-to-all | bytes 262144 | tf_op jit(solution)/shard_map/all_to_all | solution.py:88
  200.0 9.1 %all-gather.2 = bf16[1024,256]{1,0:T(8,128)(2,1)S(1)} all-gather(bf16[128,256]{1,0:T(8,128)(2,1)S(1)} %gather_fusion.12), channel_id=4, replica_groups=mesh['row'=8,'col'=4] {'row'}, dimensions={0}, use_global_device_ids=true | all-gather | bytes 589824 | tf_op jit(solution)/shard_map/all_gather | solution.py:97
  210.4 1.9 fusion.56
  215.4 20.1 %reduce-scatter.11.cloned.1.call-done = f32[128,256]{0,1:T(8,128)} async-done(((f32[512,256]{0,1:T(8,128)}), f32[128,256]{0,1:T(8,128)}) %reduce-scatter.11.cloned.1.call-update) | async-done | bytes 131088 | tf_op jit(solution)/shard_map/reduce_scatter | solution.py:98
  238.2 4.6 all-to-all-start.5
  243.0 2.6 pad_maximum_fusion.2
  245.6 3.8 gather_fusion.10
  249.4 5.1 fusion.61
  254.6 4.7 gather_fusion.14
  259.3 3.4 multiply_reduce_fusion.1
  262.7 40.4 %psum.14 = f32[256]{0:T(256)S(1)} all-reduce(f32[256]{0:T(256)S(1)} %get-tuple-element.13), channel_id=1, replica_groups=mesh['row'=8,'col'=4] {'row','col'}, use_global_device_ids=true, to_apply=%region_8.9 | all-reduce | flops 256 | bytes 2048 | tf_op jit(solution)/shard_map/psum | solution.py:123
  303.1 2.3 fusion.47
  306.6 12.7 %all_to_all.62 = bf16[32,8,256]{2,1,0:T(8,128)(2,1)S(1)} all-to-all(bf16[32,8,256]{2,1,0:T(8,128)(2,1)S(1)} %bitcast.217), channel_id=1, replica_groups=mesh['row'=8,'col'=4] {'row','col'}, dimensions={0} | all-to-all | bytes 262144 | tf_op jit(solution)/shard_map/all_to_all | solution.py:88
  320.1 9.1 %all-gather.3 = bf16[1024,256]{1,0:T(8,128)(2,1)S(1)} all-gather(bf16[128,256]{1,0:T(8,128)(2,1)S(1)} %gather_fusion.17), channel_id=5, replica_groups=mesh['row'=8,'col'=4] {'row'}, dimensions={0}, use_global_device_ids=true | all-gather | bytes 589824 | tf_op jit(solution)/shard_map/all_gather | solution.py:97
  330.6 1.9 fusion.55
  335.5 20.1 %reduce-scatter.13.cloned.1.call-done = f32[128,256]{0,1:T(8,128)} async-done(((f32[512,256]{0,1:T(8,128)}), f32[128,256]{0,1:T(8,128)}) %reduce-scatter.13.cloned.1.call-update) | async-done | bytes 131088 | tf_op jit(solution)/shard_map/reduce_scatter | solution.py:98
  358.3 4.6 all-to-all-start.7
  363.0 2.6 pad_maximum_fusion.3
  365.6 3.8 gather_fusion.15
  369.4 5.1 fusion.62
  374.5 4.7 gather_fusion.19
  379.3 3.1 fusion.45
  383.5 14.0 %all_to_all.63 = bf16[32,8,256]{2,1,0:T(8,128)(2,1)S(1)} all-to-all(bf16[32,8,256]{2,1,0:T(8,128)(2,1)S(1)} %bitcast.218), channel_id=1, replica_groups=mesh['row'=8,'col'=4] {'row','col'}, dimensions={0} | all-to-all | bytes 262144 | tf_op jit(solution)/shard_map/all_to_all | solution.py:88
  398.4 9.3 %all-gather.4 = bf16[1024,256]{1,0:T(8,128)(2,1)S(1)} all-gather(bf16[128,256]{1,0:T(8,128)(2,1)S(1)} %gather_fusion.22), channel_id=6, replica_groups=mesh['row'=8,'col'=4] {'row'}, dimensions={0}, use_global_device_ids=true | all-gather | bytes 589824 | tf_op jit(solution)/shard_map/all_gather | solution.py:97
  409.0 1.9 fusion.54
  414.0 20.1 %reduce-scatter.15.cloned.1.call-done = f32[128,256]{0,1:T(8,128)} async-done(((f32[512,256]{0,1:T(8,128)}), f32[128,256]{0,1:T(8,128)}) %reduce-scatter.15.cloned.1.call-update) | async-done | bytes 131088 | tf_op jit(solution)/shard_map/reduce_scatter | solution.py:98
  436.7 4.6 all-to-all-start.9
  441.5 2.6 pad_maximum_fusion.4
  444.1 3.8 gather_fusion.20
  447.8 5.1 fusion.63
  453.0 4.7 gather_fusion.24
  457.7 3.4 fusion.43
  462.3 14.0 %all_to_all.64 = bf16[32,8,256]{2,1,0:T(8,128)(2,1)S(1)} all-to-all(bf16[32,8,256]{2,1,0:T(8,128)(2,1)S(1)} %bitcast.214), channel_id=1, replica_groups=mesh['row'=8,'col'=4] {'row','col'}, dimensions={0} | all-to-all | bytes 262144 | tf_op jit(solution)/shard_map/all_to_all | solution.py:88
  477.2 9.1 %all-gather.5 = bf16[1024,256]{1,0:T(8,128)(2,1)S(1)} all-gather(bf16[128,256]{1,0:T(8,128)(2,1)S(1)} %gather_fusion.27), channel_id=7, replica_groups=mesh['row'=8,'col'=4] {'row'}, dimensions={0}, use_global_device_ids=true | all-gather | bytes 589824 | tf_op jit(solution)/shard_map/all_gather | solution.py:97
  491.8 21.1 %reduce-scatter.17.cloned.1.call-done = f32[128,256]{0,1:T(8,128)} async-done(((f32[512,256]{0,1:T(8,128)}), f32[128,256]{0,1:T(8,128)}) %reduce-scatter.17.cloned.1.call-update) | async-done | bytes 131088 | tf_op jit(solution)/shard_map/reduce_scatter | solution.py:98
  515.5 4.3 all-to-all-start.11
  519.8 2.5 pad_maximum_fusion.5
  522.3 3.8 gather_fusion.25
  526.1 5.1 fusion.64
  531.3 4.7 gather_fusion.29
  536.0 2.5 multiply_reduce_fusion
  538.5 40.5 %psum.15 = f32[256]{0:T(256)S(1)} all-reduce(f32[256]{0:T(256)S(1)} %get-tuple-element.5), channel_id=1, replica_groups=mesh['row'=8,'col'=4] {'row','col'}, use_global_device_ids=true, to_apply=%region_13.14 | all-reduce | flops 256 | bytes 2048 | tf_op jit(solution)/shard_map/psum | solution.py:123
  (127 shorter events, 63.8 us)
Async XLA Ops:
  6.5 85.4 %copy-start = (f32[8,3,128,128]{3,2,1,0:T(8,128)S(1)}, f32[8,3,128,128]{3,2,1,0:T(8,128)}, u32[]{:S(2)}) copy-start(f32[8,3,128,128]{3,2,1,0:T(8,128)} %param.8) | copy-start | bytes 4718596
  26.3 17.1 %copy-start.2 = (s32[8,3]{0,1:T(4,128)S(1)}, s32[8,3]{0,1:T(4,128)}, u32[]{:S(2)}) copy-start(s32[8,3]{0,1:T(4,128)} %param.9) | copy-start | bytes 292
  26.4 32.3 %copy-start.1 = (bf16[512,1024]{1,0:T(8,128)(2,1)S(1)}, bf16[512,1024]{1,0:T(8,128)(2,1)}, u32[]{:S(2)}) copy-start(bf16[512,1024]{1,0:T(8,128)(2,1)} %param.11) | copy-start | bytes 3145732
  28.2 15.7 %all-to-all-start = ((bf16[32,8,256]{2,1,0:T(8,128)(2,1)}), bf16[32,8,256]{2,1,0:T(8,128)(2,1)S(1)}, u32[]{:S(2)}, u32[]{:S(2)}) async-start(bf16[32,8,256]{2,1,0:T(8,128)(2,1)} %bitcast.8), calls=%async_computation | async-start | bytes 262144 | tf_op jit(solution)/shard_map/all_to_all | solution.py:88
  35.5 44.4 %reduce-scatter.7.cloned.1.call-start = ((), (), s32[]{:S(2)}) async-start(), calls=%async_computation.18 | async-start | bytes 655360 | tf_op jit(solution)/shard_map/reduce_scatter | solution.py:98
  37.4 48.1 %collective-permute-start = (f32[256,256]{1,0:T(8,128)}, f32[256,256]{1,0:T(8,128)S(1)}, u32[]{:S(2)}, u32[]{:S(2)}) collective-permute-start(f32[256,256]{1,0:T(8,128)} %get-tuple-element.31), channel_id=1, source_target_pairs={{0,1},{1,2},{2,3},{3,4},{4,5},{5,6},{6,7},{7,8},{8,9},{9,10},{10,1... | collective-permute-start | bytes 786440 | tf_op jit(solution)/shard_map/ppermute | solution.py:15
  41.1 44.4 %collective-permute-start.1 = (f32[256,256]{1,0:T(8,128)}, f32[256,256]{1,0:T(8,128)}, u32[]{:S(2)}, u32[]{:S(2)}) collective-permute-start(f32[256,256]{1,0:T(8,128)} %get-tuple-element.32), channel_id=1, source_target_pairs={{1,0},{2,1},{3,2},{4,3},{5,4},{6,5},{7,6},{8,7},{9,8},{10,9},{11,1... | collective-permute-start | bytes 786440 | tf_op jit(solution)/shard_map/ppermute | solution.py:18
  44.8 15.4 %copy-start.3 = (s32[256]{0:T(256)S(1)}, s32[256]{0:T(256)}, u32[]{:S(2)}) copy-start(s32[256]{0:T(256)} %param.13) | copy-start | bytes 3076
  44.8 15.4 %copy-start.4 = (s32[256]{0:T(256)S(1)}, s32[256]{0:T(256)}, u32[]{:S(2)}) copy-start(s32[256]{0:T(256)} %param.12) | copy-start | bytes 3076
  82.6 14.5 %all-to-all-start.1 = ((f32[32,8,256]{2,1,0:T(8,128)}), f32[32,8,256]{2,1,0:T(8,128)S(1)}, u32[]{:S(2)}, u32[]{:S(2)}) async-start(f32[32,8,256]{2,1,0:T(8,128)} %bitcast.15), calls=%async_computation.2 | async-start | bytes 524288 | tf_op jit(solution)/shard_map/all_to_all | solution.py:101
  85.5 71.3 %reduce-scatter.9.cloned.1.call-start = ((), (), s32[]{:S(2)}) async-start(), calls=%async_computation.19 | async-start | bytes 655360 | tf_op jit(solution)/shard_map/reduce_scatter | solution.py:98
  133.6 30.5 %collective-permute-start.2 = (f32[256,256]{1,0:T(8,128)}, f32[256,256]{1,0:T(8,128)S(1)}, u32[]{:S(2)}, u32[]{:S(2)}) collective-permute-start(f32[256,256]{1,0:T(8,128)} %get-tuple-element.29), channel_id=1, source_target_pairs={{0,1},{1,2},{2,3},{3,4},{4,5},{5,6},{6,7},{7,8},{8,9},{9,10},{10,1... | collective-permute-start | bytes 786440 | tf_op jit(solution)/shard_map/ppermute | solution.py:15
  135.4 28.8 %collective-permute-start.3 = (f32[256,256]{1,0:T(8,128)}, f32[256,256]{1,0:T(8,128)}, u32[]{:S(2)}, u32[]{:S(2)}) collective-permute-start(f32[256,256]{1,0:T(8,128)} %get-tuple-element.30), channel_id=1, source_target_pairs={{1,0},{2,1},{3,2},{4,3},{5,4},{6,5},{7,6},{8,7},{9,8},{10,9},{11,1... | collective-permute-start | bytes 786440 | tf_op jit(solution)/shard_map/ppermute | solution.py:18
  159.5 16.3 %all-to-all-start.3 = ((f32[32,8,256]{2,1,0:T(8,128)}), f32[32,8,256]{2,1,0:T(8,128)S(1)}, u32[]{:S(2)}, u32[]{:S(2)}) async-start(f32[32,8,256]{2,1,0:T(8,128)} %bitcast.27), calls=%async_computation.5 | async-start | bytes 524288 | tf_op jit(solution)/shard_map/all_to_all | solution.py:101
  164.1 71.3 %reduce-scatter.11.cloned.1.call-start = ((), (), s32[]{:S(2)}) async-start(), calls=%async_computation.20 | async-start | bytes 655360 | tf_op jit(solution)/shard_map/reduce_scatter | solution.py:98
  212.3 30.7 %collective-permute-start.4 = (f32[256,256]{1,0:T(8,128)}, f32[256,256]{1,0:T(8,128)S(1)}, u32[]{:S(2)}, u32[]{:S(2)}) collective-permute-start(f32[256,256]{1,0:T(8,128)} %get-tuple-element.27), channel_id=1, source_target_pairs={{0,1},{1,2},{2,3},{3,4},{4,5},{5,6},{6,7},{7,8},{8,9},{9,10},{10,1... | collective-permute-start | bytes 786440 | tf_op jit(solution)/shard_map/ppermute | solution.py:15
  214.1 28.9 %collective-permute-start.5 = (f32[256,256]{1,0:T(8,128)}, f32[256,256]{1,0:T(8,128)}, u32[]{:S(2)}, u32[]{:S(2)}) collective-permute-start(f32[256,256]{1,0:T(8,128)} %get-tuple-element.28), channel_id=1, source_target_pairs={{1,0},{2,1},{3,2},{4,3},{5,4},{6,5},{7,6},{8,7},{9,8},{10,9},{11,1... | collective-permute-start | bytes 786440 | tf_op jit(solution)/shard_map/ppermute | solution.py:18
  238.2 16.4 %all-to-all-start.5 = ((f32[32,8,256]{2,1,0:T(8,128)}), f32[32,8,256]{2,1,0:T(8,128)S(1)}, u32[]{:S(2)}, u32[]{:S(2)}) async-start(f32[32,8,256]{2,1,0:T(8,128)} %bitcast.38), calls=%async_computation.8 | async-start | bytes 524288 | tf_op jit(solution)/shard_map/all_to_all | solution.py:101
  242.8 112.8 %reduce-scatter.13.cloned.1.call-start = ((), (), s32[]{:S(2)}) async-start(), calls=%async_computation.21 | async-start | bytes 655360 | tf_op jit(solution)/shard_map/reduce_scatter | solution.py:98
  332.5 30.5 %collective-permute-start.6 = (f32[256,256]{1,0:T(8,128)}, f32[256,256]{1,0:T(8,128)S(1)}, u32[]{:S(2)}, u32[]{:S(2)}) collective-permute-start(f32[256,256]{1,0:T(8,128)} %get-tuple-element.25), channel_id=1, source_target_pairs={{0,1},{1,2},{2,3},{3,4},{4,5},{5,6},{6,7},{7,8},{8,9},{9,10},{10,1... | collective-permute-start | bytes 786440 | tf_op jit(solution)/shard_map/ppermute | solution.py:15
  334.2 28.8 %collective-permute-start.7 = (f32[256,256]{1,0:T(8,128)}, f32[256,256]{1,0:T(8,128)}, u32[]{:S(2)}, u32[]{:S(2)}) collective-permute-start(f32[256,256]{1,0:T(8,128)} %get-tuple-element.26), channel_id=1, source_target_pairs={{1,0},{2,1},{3,2},{4,3},{5,4},{6,5},{7,6},{8,7},{9,8},{10,9},{11,1... | collective-permute-start | bytes 786440 | tf_op jit(solution)/shard_map/ppermute | solution.py:18
  358.3 16.2 %all-to-all-start.7 = ((f32[32,8,256]{2,1,0:T(8,128)}), f32[32,8,256]{2,1,0:T(8,128)S(1)}, u32[]{:S(2)}, u32[]{:S(2)}) async-start(f32[32,8,256]{2,1,0:T(8,128)} %bitcast.49), calls=%async_computation.11 | async-start | bytes 524288 | tf_op jit(solution)/shard_map/all_to_all | solution.py:101
  362.9 71.1 %reduce-scatter.15.cloned.1.call-start = ((), (), s32[]{:S(2)}) async-start(), calls=%async_computation.22 | async-start | bytes 655360 | tf_op jit(solution)/shard_map/reduce_scatter | solution.py:98
  410.9 30.5 %collective-permute-start.8 = (f32[256,256]{1,0:T(8,128)}, f32[256,256]{1,0:T(8,128)S(1)}, u32[]{:S(2)}, u32[]{:S(2)}) collective-permute-start(f32[256,256]{1,0:T(8,128)} %get-tuple-element.23), channel_id=1, source_target_pairs={{0,1},{1,2},{2,3},{3,4},{4,5},{5,6},{6,7},{7,8},{8,9},{9,10},{10,1... | collective-permute-start | bytes 786440 | tf_op jit(solution)/shard_map/ppermute | solution.py:15
  412.7 28.7 %collective-permute-start.9 = (f32[256,256]{1,0:T(8,128)}, f32[256,256]{1,0:T(8,128)}, u32[]{:S(2)}, u32[]{:S(2)}) collective-permute-start(f32[256,256]{1,0:T(8,128)} %get-tuple-element.24), channel_id=1, source_target_pairs={{1,0},{2,1},{3,2},{4,3},{5,4},{6,5},{7,6},{8,7},{9,8},{10,9},{11,1... | collective-permute-start | bytes 786440 | tf_op jit(solution)/shard_map/ppermute | solution.py:18
  436.7 16.2 %all-to-all-start.9 = ((f32[32,8,256]{2,1,0:T(8,128)}), f32[32,8,256]{2,1,0:T(8,128)S(1)}, u32[]{:S(2)}, u32[]{:S(2)}) async-start(f32[32,8,256]{2,1,0:T(8,128)} %bitcast.60), calls=%async_computation.14 | async-start | bytes 524288 | tf_op jit(solution)/shard_map/all_to_all | solution.py:101
  441.4 71.5 %reduce-scatter.17.cloned.1.call-start = ((), (), s32[]{:S(2)}) async-start(), calls=%async_computation.23 | async-start | bytes 655360 | tf_op jit(solution)/shard_map/reduce_scatter | solution.py:98
  488.7 31.2 %collective-permute-start.10 = (f32[256,256]{1,0:T(8,128)S(1)}, f32[256,256]{1,0:T(8,128)S(1)}, u32[]{:S(2)}, u32[]{:S(2)}) collective-permute-start(f32[256,256]{1,0:T(8,128)S(1)} %get-tuple-element.21), channel_id=1, source_target_pairs={{0,1},{1,2},{2,3},{3,4},{4,5},{5,6},{6,7},{7,8},{8,9},{9,10},{10,1... | collective-permute-start | bytes 786440 | tf_op jit(solution)/shard_map/ppermute | solution.py:15
  490.5 29.4 %collective-permute-start.11 = (f32[256,256]{1,0:T(8,128)S(1)}, f32[256,256]{1,0:T(8,128)S(1)}, u32[]{:S(2)}, u32[]{:S(2)}) collective-permute-start(f32[256,256]{1,0:T(8,128)S(1)} %get-tuple-element.22), channel_id=1, source_target_pairs={{1,0},{2,1},{3,2},{4,3},{5,4},{6,5},{7,6},{8,7},{9,8},{10,9},{11,1... | collective-permute-start | bytes 786440 | tf_op jit(solution)/shard_map/ppermute | solution.py:18
  515.5 15.7 %all-to-all-start.11 = ((f32[32,8,256]{2,1,0:T(8,128)}), f32[32,8,256]{2,1,0:T(8,128)S(1)}, u32[]{:S(2)}, u32[]{:S(2)}) async-start(f32[32,8,256]{2,1,0:T(8,128)} %bitcast.71), calls=%async_computation.17 | async-start | bytes 524288 | tf_op jit(solution)/shard_map/all_to_all | solution.py:101
Sparse Core Ops, SparseCore 0:
  60.1 19.7 reduce-scatter.6
  131.9 24.8 reduce-scatter.8
  210.5 24.8 reduce-scatter.10
  330.7 24.8 reduce-scatter.12
  409.1 24.8 reduce-scatter.14
  487.7 25.0 reduce-scatter.16
where the time goes:
time: 597 us; the launch traced here: 587 us
  blocking collectives  210 us (35%)
  local copies, waits for them, and re-layouts  123 us (21%)
  waiting for transfers between devices  106 us (18%)
  starting transfers between devices  53.7 us (9%)
  other arithmetic  42.1 us (7%)
  matrix products  38.6 us (6%)
  between operations  14.5 us (2%)
    reduce_scatter x6, waiting for transfers between devices, fluid_loads(): lax.psum_scatter(partial_value, 'col', scatter_dimension=0, tiled=True)  105 us
    psum x2, blocking collectives, body(): squares = lax.psum(jnp.sum(current * current, axis=0), ('row', 'col'))  80.9 us
    all_to_all x5, blocking collectives, fluid_loads(): lax.all_to_all(outgoing.reshape(devices, slot_count, mode_width), ('row',...  68.7 us
    all_gather x6, blocking collectives, fluid_loads(): lax.all_gather(wetted, 'row', axis=0, tiled=True)  60.2 us
    dot_general x6, matrix products, stiffness(): jnp.einsum('rkij,rkjn->rin', k_blocks, chosen, precision=lax.Precision.HI...  30.9 us
    gather x6, local copies, waits for them, and re-layouts, fluid_loads(): return padded_sum[return_index]  28.2 us
    all_to_all x6, starting transfers between devices, fluid_loads(): lax.all_to_all(sending, ('row', 'col'), split_axis=0, concat_axis=0, tile...  25.7 us
    gather x6, local copies, waits for them, and re-layouts, stiffness(): chosen = pieces[local_cols]  22.7 us
  transfers between devices with their start and end apart: 25, of which 7 were waited for; matrix products, arithmetic and copies ran while one was open for 20% of the time, Pallas kernels for 0%

commit v1 on v0

--- a/solution.py
+++ b/solution.py
@@ -120,7 +120,7 @@
             following = 2.0 * (operate(current) - centre * current) / radius - previous
             previous = current
             current = following
-        squares = lax.psum(jnp.sum(current * current, axis=0), ("row", "col"))
+        squares = lax.psum(lax.psum(jnp.sum(current * current, axis=0), "col"), "row")
         current = current / jnp.sqrt(squares / total_rows + 1e-06)
     return current
 

time: 597 us -> 562 us (0.941)
  blocking collectives: 210 us -> 174 us
    psum x2 -> x4, blocking collectives: 80.9 us -> 47.9 us  [the longest x2 24.1 us: body(): lax.psum(jnp.sum(current * current, axis=0), 'col')]
  transfers between devices with their start and end apart: 25 -> 25, of which waited for: 7 -> 7; matrix products, arithmetic and copies ran while one was open for 20% -> 21% of each run, Pallas kernels for 0% -> 0%
where the time goes in v1:
time: 562 us; the launch traced here: 551 us
  blocking collectives  174 us (31%)
  local copies, waits for them, and re-layouts  123 us (22%)
  waiting for transfers between devices  106 us (19%)
  starting transfers between devices  53.7 us (10%)
  other arithmetic  42 us (7%)
  matrix products  38.8 us (7%)
  between operations  14.4 us (3%)
    reduce_scatter x6, waiting for transfers between devices, fluid_loads(): lax.psum_scatter(partial_value, 'col', scatter_dimension=0, tiled=True)  105 us
    all_to_all x5, blocking collectives, fluid_loads(): lax.all_to_all(outgoing.reshape(devices, slot_count, mode_width), ('row',...  66.2 us
    all_gather x6, blocking collectives, fluid_loads(): lax.all_gather(wetted, 'row', axis=0, tiled=True)  60 us
    dot_general x6, matrix products, stiffness(): jnp.einsum('rkij,rkjn->rin', k_blocks, chosen, precision=lax.Precision.HI...  31.1 us
    gather x6, local copies, waits for them, and re-layouts, fluid_loads(): return padded_sum[return_index]  28.1 us
    all_to_all x6, starting transfers between devices, fluid_loads(): lax.all_to_all(sending, ('row', 'col'), split_axis=0, concat_axis=0, tile...  25.7 us
    psum x2, blocking collectives, body(): lax.psum(jnp.sum(current * current, axis=0), 'col')  24.1 us
    psum x2, blocking collectives, body(): lax.psum(lax.psum(jnp.sum(current * current, axis=0), 'col'), 'row')  23.8 us
  transfers between devices with their start and end apart: 25, of which 7 were waited for; matrix products, arithmetic and copies ran while one was open for 21% of the time, Pallas kernels for 0%

profile of v1, /device:TPU:0, one launch (start us, length us, event | category | flops | bytes accessed | tf_op | source)
XLA Modules:
  0.0 551.4 jit_solution(9457661289626836668)
XLA Ops:
  9.5 15.5 %scatter_custom_fusion = s32[256]{0:T(256)S(1)} fusion(s32[4096]{0:T(1024)S(1)} %get-tuple-element.35, s32[4096]{0:T(1024)S(1)} %get-tuple-element.20, s32[]{:T(128)} %constant.94.clone.1), kind=kCustom, calls=%fused_computation.139 | custom fusion | bytes 1028 | tf_op jit(solution)/shard_map/scatter | solution.py:50
  28.2 7.3 %all-to-all-start = ((bf16[32,8,256]{2,1,0:T(8,128)(2,1)}), bf16[32,8,256]{2,1,0:T(8,128)(2,1)S(1)}, u32[]{:S(2)}, u32[]{:S(2)}) async-start(bf16[32,8,256]{2,1,0:T(8,128)(2,1)} %bitcast.8), calls=%async_computation | async-start | bytes 262144 | tf_op jit(solution)/shard_map/all_to_all | solution.py:88
  37.5 3.7 collective-permute-start
  44.8 13.9 %all-gather = bf16[1024,256]{1,0:T(8,128)(2,1)S(1)} all-gather(bf16[128,256]{1,0:T(8,128)(2,1)S(1)} %gather_fusion.2), channel_id=2, replica_groups=mesh['row'=8,'col'=4] {'row'}, dimensions={0}, use_global_device_ids=true | all-gather | bytes 589824 | tf_op jit(solution)/shard_map/all_gather | solution.py:97
  60.3 15.5 %scatter_custom_fusion.2 = s32[1024]{0:T(1024)S(1)} fusion(s32[4096]{0:T(1024)S(1)} %get-tuple-element.19, s32[4096]{0:T(1024)S(1)} %add_bitcast_fusion, s32[]{:T(128)} %constant.101.clone.1), kind=kCustom, calls=%fused_computation.110 | custom fusion | bytes 4100 | tf_op jit(solution)/shard_map/scatter | solution.py:53
  75.8 4.1 reduce-scatter.7.cloned.1.call-done
  82.6 2.9 all-to-all-start.1
  85.6 2.6 pad_maximum_fusion
  88.1 3.8 gather_fusion
  92.0 5.2 fusion.59
  97.2 4.7 gather_fusion.4
  101.8 3.0 fusion.51
  106.1 14.0 %all_to_all.60 = bf16[32,8,256]{2,1,0:T(8,128)(2,1)S(1)} all-to-all(bf16[32,8,256]{2,1,0:T(8,128)(2,1)S(1)} %bitcast.215), channel_id=1, replica_groups=mesh['row'=8,'col'=4] {'row','col'}, dimensions={0} | all-to-all | bytes 262144 | tf_op jit(solution)/shard_map/all_to_all | solution.py:88
  120.9 9.6 %all-gather.1 = bf16[1024,256]{1,0:T(8,128)(2,1)S(1)} all-gather(bf16[128,256]{1,0:T(8,128)(2,1)S(1)} %gather_fusion.7), channel_id=3, replica_groups=mesh['row'=8,'col'=4] {'row'}, dimensions={0}, use_global_device_ids=true | all-gather | bytes 589824 | tf_op jit(solution)/shard_map/all_gather | solution.py:97
  131.8 1.9 fusion.57
  136.8 20.0 %reduce-scatter.9.cloned.1.call-done = f32[128,256]{0,1:T(8,128)} async-done(((f32[512,256]{0,1:T(8,128)}), f32[128,256]{0,1:T(8,128)}) %reduce-scatter.9.cloned.1.call-update) | async-done | bytes 131088 | tf_op jit(solution)/shard_map/reduce_scatter | solution.py:98
  159.5 4.7 all-to-all-start.3
  164.3 2.6 pad_maximum_fusion.1
  166.9 3.8 gather_fusion.5
  170.7 5.2 fusion.60
  175.9 4.7 gather_fusion.9
  180.6 3.4 fusion.49
  185.2 14.0 %all_to_all.61 = bf16[32,8,256]{2,1,0:T(8,128)(2,1)S(1)} all-to-all(bf16[32,8,256]{2,1,0:T(8,128)(2,1)S(1)} %bitcast.216), channel_id=1, replica_groups=mesh['row'=8,'col'=4] {'row','col'}, dimensions={0} | all-to-all | bytes 262144 | tf_op jit(solution)/shard_map/all_to_all | solution.py:88
  200.1 9.1 %all-gather.2 = bf16[1024,256]{1,0:T(8,128)(2,1)S(1)} all-gather(bf16[128,256]{1,0:T(8,128)(2,1)S(1)} %gather_fusion.12), channel_id=4, replica_groups=mesh['row'=8,'col'=4] {'row'}, dimensions={0}, use_global_device_ids=true | all-gather | bytes 589824 | tf_op jit(solution)/shard_map/all_gather | solution.py:97
  215.4 20.1 %reduce-scatter.11.cloned.1.call-done = f32[128,256]{0,1:T(8,128)} async-done(((f32[512,256]{0,1:T(8,128)}), f32[128,256]{0,1:T(8,128)}) %reduce-scatter.11.cloned.1.call-update) | async-done | bytes 131088 | tf_op jit(solution)/shard_map/reduce_scatter | solution.py:98
  238.2 4.7 all-to-all-start.5
  242.9 2.6 pad_maximum_fusion.2
  245.5 3.8 gather_fusion.10
  249.3 5.2 fusion.61
  254.5 4.7 gather_fusion.14
  259.2 3.4 multiply_reduce_fusion.1
  262.6 12.1 %psum.28 = f32[256]{0:T(256)S(1)} all-reduce(f32[256]{0:T(256)S(1)} %get-tuple-element.13), channel_id=1, replica_groups=mesh['row'=8,'col'=4] {'col'}, use_global_device_ids=true, to_apply=%region_8.9 | all-reduce | flops 256 | bytes 2048 | tf_op jit(solution)/shard_map/psum | solution.py:123
  274.7 11.9 %psum.29 = f32[256]{0:T(256)S(1)} all-reduce(f32[256]{0:T(256)S(1)} %psum.28), channel_id=1, replica_groups=mesh['row'=8,'col'=4] {'row'}, use_global_device_ids=true, to_apply=%region_9.10 | all-reduce | flops 256 | bytes 2048 | tf_op jit(solution)/shard_map/psum | solution.py:123
  286.6 2.3 fusion.47
  290.1 10.1 %all_to_all.62 = bf16[32,8,256]{2,1,0:T(8,128)(2,1)S(1)} all-to-all(bf16[32,8,256]{2,1,0:T(8,128)(2,1)S(1)} %bitcast.217), channel_id=1, replica_groups=mesh['row'=8,'col'=4] {'row','col'}, dimensions={0} | all-to-all | bytes 262144 | tf_op jit(solution)/shard_map/all_to_all | solution.py:88
  301.1 9.1 %all-gather.3 = bf16[1024,256]{1,0:T(8,128)(2,1)S(1)} all-gather(bf16[128,256]{1,0:T(8,128)(2,1)S(1)} %gather_fusion.17), channel_id=5, replica_groups=mesh['row'=8,'col'=4] {'row'}, dimensions={0}, use_global_device_ids=true | all-gather | bytes 589824 | tf_op jit(solution)/shard_map/all_gather | solution.py:97
  311.5 1.9 fusion.55
  316.5 20.1 %reduce-scatter.13.cloned.1.call-done = f32[128,256]{0,1:T(8,128)} async-done(((f32[512,256]{0,1:T(8,128)}), f32[128,256]{0,1:T(8,128)}) %reduce-scatter.13.cloned.1.call-update) | async-done | bytes 131088 | tf_op jit(solution)/shard_map/reduce_scatter | solution.py:98
  339.2 4.6 all-to-all-start.7
  343.9 2.6 pad_maximum_fusion.3
  346.5 3.8 gather_fusion.15
  350.3 5.2 fusion.62
  355.5 4.7 gather_fusion.19
  360.2 3.1 fusion.45
  364.5 14.0 %all_to_all.63 = bf16[32,8,256]{2,1,0:T(8,128)(2,1)S(1)} all-to-all(bf16[32,8,256]{2,1,0:T(8,128)(2,1)S(1)} %bitcast.218), channel_id=1, replica_groups=mesh['row'=8,'col'=4] {'row','col'}, dimensions={0} | all-to-all | bytes 262144 | tf_op jit(solution)/shard_map/all_to_all | solution.py:88
  379.3 9.1 %all-gather.4 = bf16[1024,256]{1,0:T(8,128)(2,1)S(1)} all-gather(bf16[128,256]{1,0:T(8,128)(2,1)S(1)} %gather_fusion.22), channel_id=6, replica_groups=mesh['row'=8,'col'=4] {'row'}, dimensions={0}, use_global_device_ids=true | all-gather | bytes 589824 | tf_op jit(solution)/shard_map/all_gather | solution.py:97
  394.7 20.0 %reduce-scatter.15.cloned.1.call-done = f32[128,256]{0,1:T(8,128)} async-done(((f32[512,256]{0,1:T(8,128)}), f32[128,256]{0,1:T(8,128)}) %reduce-scatter.15.cloned.1.call-update) | async-done | bytes 131088 | tf_op jit(solution)/shard_map/reduce_scatter | solution.py:98
  417.4 4.7 all-to-all-start.9
  422.4 2.6 pad_maximum_fusion.4
  425.0 3.8 gather_fusion.20
  428.8 5.2 fusion.63
  434.0 4.7 gather_fusion.24
  438.7 3.4 fusion.43
  443.3 14.0 %all_to_all.64 = bf16[32,8,256]{2,1,0:T(8,128)(2,1)S(1)} all-to-all(bf16[32,8,256]{2,1,0:T(8,128)(2,1)S(1)} %bitcast.214), channel_id=1, replica_groups=mesh['row'=8,'col'=4] {'row','col'}, dimensions={0} | all-to-all | bytes 262144 | tf_op jit(solution)/shard_map/all_to_all | solution.py:88
  458.1 9.1 %all-gather.5 = bf16[1024,256]{1,0:T(8,128)(2,1)S(1)} all-gather(bf16[128,256]{1,0:T(8,128)(2,1)S(1)} %gather_fusion.27), channel_id=7, replica_groups=mesh['row'=8,'col'=4] {'row'}, dimensions={0}, use_global_device_ids=true | all-gather | bytes 589824 | tf_op jit(solution)/shard_map/all_gather | solution.py:97
  472.7 21.1 %reduce-scatter.17.cloned.1.call-done = f32[128,256]{0,1:T(8,128)} async-done(((f32[512,256]{0,1:T(8,128)}), f32[128,256]{0,1:T(8,128)}) %reduce-scatter.17.cloned.1.call-update) | async-done | bytes 131088 | tf_op jit(solution)/shard_map/reduce_scatter | solution.py:98
  496.5 4.2 all-to-all-start.11
  500.7 2.5 pad_maximum_fusion.5
  503.2 3.8 gather_fusion.25
  507.0 5.2 fusion.64
  512.2 4.7 gather_fusion.29
  516.9 2.5 multiply_reduce_fusion
  519.3 12.0 %psum.30 = f32[256]{0:T(256)S(1)} all-reduce(f32[256]{0:T(256)S(1)} %get-tuple-element.5), channel_id=1, replica_groups=mesh['row'=8,'col'=4] {'col'}, use_global_device_ids=true, to_apply=%region_14.15 | all-reduce | flops 256 | bytes 2048 | tf_op jit(solution)/shard_map/psum | solution.py:123
  531.3 11.9 %psum.31 = f32[256]{0:T(256)S(1)} all-reduce(f32[256]{0:T(256)S(1)} %psum.30), channel_id=1, replica_groups=mesh['row'=8,'col'=4] {'row'}, use_global_device_ids=true, to_apply=%region_15.16 | all-reduce | flops 256 | bytes 2048 | tf_op jit(solution)/shard_map/psum | solution.py:123
  (129 shorter events, 67.6 us)
Async XLA Ops:
  6.5 85.4 %copy-start = (f32[8,3,128,128]{3,2,1,0:T(8,128)S(1)}, f32[8,3,128,128]{3,2,1,0:T(8,128)}, u32[]{:S(2)}) copy-start(f32[8,3,128,128]{3,2,1,0:T(8,128)} %param.8) | copy-start | bytes 4718596
  26.3 17.2 %copy-start.2 = (s32[8,3]{0,1:T(4,128)S(1)}, s32[8,3]{0,1:T(4,128)}, u32[]{:S(2)}) copy-start(s32[8,3]{0,1:T(4,128)} %param.9) | copy-start | bytes 292
  26.4 32.3 %copy-start.1 = (bf16[512,1024]{1,0:T(8,128)(2,1)S(1)}, bf16[512,1024]{1,0:T(8,128)(2,1)}, u32[]{:S(2)}) copy-start(bf16[512,1024]{1,0:T(8,128)(2,1)} %param.11) | copy-start | bytes 3145732
  28.2 15.7 %all-to-all-start = ((bf16[32,8,256]{2,1,0:T(8,128)(2,1)}), bf16[32,8,256]{2,1,0:T(8,128)(2,1)S(1)}, u32[]{:S(2)}, u32[]{:S(2)}) async-start(bf16[32,8,256]{2,1,0:T(8,128)(2,1)} %bitcast.8), calls=%async_computation | async-start | bytes 262144 | tf_op jit(solution)/shard_map/all_to_all | solution.py:88
  35.5 44.4 %reduce-scatter.7.cloned.1.call-start = ((), (), s32[]{:S(2)}) async-start(), calls=%async_computation.18 | async-start | bytes 655360 | tf_op jit(solution)/shard_map/reduce_scatter | solution.py:98
  37.5 48.1 %collective-permute-start = (f32[256,256]{1,0:T(8,128)}, f32[256,256]{1,0:T(8,128)S(1)}, u32[]{:S(2)}, u32[]{:S(2)}) collective-permute-start(f32[256,256]{1,0:T(8,128)} %get-tuple-element.31), channel_id=1, source_target_pairs={{0,1},{1,2},{2,3},{3,4},{4,5},{5,6},{6,7},{7,8},{8,9},{9,10},{10,1... | collective-permute-start | bytes 786440 | tf_op jit(solution)/shard_map/ppermute | solution.py:15
  41.1 44.4 %collective-permute-start.1 = (f32[256,256]{1,0:T(8,128)}, f32[256,256]{1,0:T(8,128)}, u32[]{:S(2)}, u32[]{:S(2)}) collective-permute-start(f32[256,256]{1,0:T(8,128)} %get-tuple-element.32), channel_id=1, source_target_pairs={{1,0},{2,1},{3,2},{4,3},{5,4},{6,5},{7,6},{8,7},{9,8},{10,9},{11,1... | collective-permute-start | bytes 786440 | tf_op jit(solution)/shard_map/ppermute | solution.py:18
  44.8 15.4 %copy-start.3 = (s32[256]{0:T(256)S(1)}, s32[256]{0:T(256)}, u32[]{:S(2)}) copy-start(s32[256]{0:T(256)} %param.13) | copy-start | bytes 3076
  44.8 15.4 %copy-start.4 = (s32[256]{0:T(256)S(1)}, s32[256]{0:T(256)}, u32[]{:S(2)}) copy-start(s32[256]{0:T(256)} %param.12) | copy-start | bytes 3076
  82.6 14.5 %all-to-all-start.1 = ((f32[32,8,256]{2,1,0:T(8,128)}), f32[32,8,256]{2,1,0:T(8,128)S(1)}, u32[]{:S(2)}, u32[]{:S(2)}) async-start(f32[32,8,256]{2,1,0:T(8,128)} %bitcast.15), calls=%async_computation.2 | async-start | bytes 524288 | tf_op jit(solution)/shard_map/all_to_all | solution.py:101
  85.5 71.3 %reduce-scatter.9.cloned.1.call-start = ((), (), s32[]{:S(2)}) async-start(), calls=%async_computation.19 | async-start | bytes 655360 | tf_op jit(solution)/shard_map/reduce_scatter | solution.py:98
  133.7 30.6 %collective-permute-start.2 = (f32[256,256]{1,0:T(8,128)}, f32[256,256]{1,0:T(8,128)S(1)}, u32[]{:S(2)}, u32[]{:S(2)}) collective-permute-start(f32[256,256]{1,0:T(8,128)} %get-tuple-element.29), channel_id=1, source_target_pairs={{0,1},{1,2},{2,3},{3,4},{4,5},{5,6},{6,7},{7,8},{8,9},{9,10},{10,1... | collective-permute-start | bytes 786440 | tf_op jit(solution)/shard_map/ppermute | solution.py:15
  135.5 28.8 %collective-permute-start.3 = (f32[256,256]{1,0:T(8,128)}, f32[256,256]{1,0:T(8,128)}, u32[]{:S(2)}, u32[]{:S(2)}) collective-permute-start(f32[256,256]{1,0:T(8,128)} %get-tuple-element.30), channel_id=1, source_target_pairs={{1,0},{2,1},{3,2},{4,3},{5,4},{6,5},{7,6},{8,7},{9,8},{10,9},{11,1... | collective-permute-start | bytes 786440 | tf_op jit(solution)/shard_map/ppermute | solution.py:18
  159.5 16.3 %all-to-all-start.3 = ((f32[32,8,256]{2,1,0:T(8,128)}), f32[32,8,256]{2,1,0:T(8,128)S(1)}, u32[]{:S(2)}, u32[]{:S(2)}) async-start(f32[32,8,256]{2,1,0:T(8,128)} %bitcast.27), calls=%async_computation.5 | async-start | bytes 524288 | tf_op jit(solution)/shard_map/all_to_all | solution.py:101
  164.2 71.3 %reduce-scatter.11.cloned.1.call-start = ((), (), s32[]{:S(2)}) async-start(), calls=%async_computation.20 | async-start | bytes 655360 | tf_op jit(solution)/shard_map/reduce_scatter | solution.py:98
  212.4 30.5 %collective-permute-start.4 = (f32[256,256]{1,0:T(8,128)}, f32[256,256]{1,0:T(8,128)S(1)}, u32[]{:S(2)}, u32[]{:S(2)}) collective-permute-start(f32[256,256]{1,0:T(8,128)} %get-tuple-element.27), channel_id=1, source_target_pairs={{0,1},{1,2},{2,3},{3,4},{4,5},{5,6},{6,7},{7,8},{8,9},{9,10},{10,1... | collective-permute-start | bytes 786440 | tf_op jit(solution)/shard_map/ppermute | solution.py:15
  214.1 28.8 %collective-permute-start.5 = (f32[256,256]{1,0:T(8,128)}, f32[256,256]{1,0:T(8,128)}, u32[]{:S(2)}, u32[]{:S(2)}) collective-permute-start(f32[256,256]{1,0:T(8,128)} %get-tuple-element.28), channel_id=1, source_target_pairs={{1,0},{2,1},{3,2},{4,3},{5,4},{6,5},{7,6},{8,7},{9,8},{10,9},{11,1... | collective-permute-start | bytes 786440 | tf_op jit(solution)/shard_map/ppermute | solution.py:18
  238.2 16.3 %all-to-all-start.5 = ((f32[32,8,256]{2,1,0:T(8,128)}), f32[32,8,256]{2,1,0:T(8,128)S(1)}, u32[]{:S(2)}, u32[]{:S(2)}) async-start(f32[32,8,256]{2,1,0:T(8,128)} %bitcast.38), calls=%async_computation.8 | async-start | bytes 524288 | tf_op jit(solution)/shard_map/all_to_all | solution.py:101
  242.9 93.7 %reduce-scatter.13.cloned.1.call-start = ((), (), s32[]{:S(2)}) async-start(), calls=%async_computation.21 | async-start | bytes 655360 | tf_op jit(solution)/shard_map/reduce_scatter | solution.py:98
  313.4 30.5 %collective-permute-start.6 = (f32[256,256]{1,0:T(8,128)}, f32[256,256]{1,0:T(8,128)S(1)}, u32[]{:S(2)}, u32[]{:S(2)}) collective-permute-start(f32[256,256]{1,0:T(8,128)} %get-tuple-element.25), channel_id=1, source_target_pairs={{0,1},{1,2},{2,3},{3,4},{4,5},{5,6},{6,7},{7,8},{8,9},{9,10},{10,1... | collective-permute-start | bytes 786440 | tf_op jit(solution)/shard_map/ppermute | solution.py:15
  315.2 28.8 %collective-permute-start.7 = (f32[256,256]{1,0:T(8,128)}, f32[256,256]{1,0:T(8,128)}, u32[]{:S(2)}, u32[]{:S(2)}) collective-permute-start(f32[256,256]{1,0:T(8,128)} %get-tuple-element.26), channel_id=1, source_target_pairs={{1,0},{2,1},{3,2},{4,3},{5,4},{6,5},{7,6},{8,7},{9,8},{10,9},{11,1... | collective-permute-start | bytes 786440 | tf_op jit(solution)/shard_map/ppermute | solution.py:18
  339.2 16.3 %all-to-all-start.7 = ((f32[32,8,256]{2,1,0:T(8,128)}), f32[32,8,256]{2,1,0:T(8,128)S(1)}, u32[]{:S(2)}, u32[]{:S(2)}) async-start(f32[32,8,256]{2,1,0:T(8,128)} %bitcast.49), calls=%async_computation.11 | async-start | bytes 524288 | tf_op jit(solution)/shard_map/all_to_all | solution.py:101
  343.9 70.9 %reduce-scatter.15.cloned.1.call-start = ((), (), s32[]{:S(2)}) async-start(), calls=%async_computation.22 | async-start | bytes 655360 | tf_op jit(solution)/shard_map/reduce_scatter | solution.py:98
  391.6 30.8 %collective-permute-start.8 = (f32[256,256]{1,0:T(8,128)}, f32[256,256]{1,0:T(8,128)S(1)}, u32[]{:S(2)}, u32[]{:S(2)}) collective-permute-start(f32[256,256]{1,0:T(8,128)} %get-tuple-element.23), channel_id=1, source_target_pairs={{0,1},{1,2},{2,3},{3,4},{4,5},{5,6},{6,7},{7,8},{8,9},{9,10},{10,1... | collective-permute-start | bytes 786440 | tf_op jit(solution)/shard_map/ppermute | solution.py:15
  393.4 29.0 %collective-permute-start.9 = (f32[256,256]{1,0:T(8,128)}, f32[256,256]{1,0:T(8,128)}, u32[]{:S(2)}, u32[]{:S(2)}) collective-permute-start(f32[256,256]{1,0:T(8,128)} %get-tuple-element.24), channel_id=1, source_target_pairs={{1,0},{2,1},{3,2},{4,3},{5,4},{6,5},{7,6},{8,7},{9,8},{10,9},{11,1... | collective-permute-start | bytes 786440 | tf_op jit(solution)/shard_map/ppermute | solution.py:18
  417.4 16.6 %all-to-all-start.9 = ((f32[32,8,256]{2,1,0:T(8,128)}), f32[32,8,256]{2,1,0:T(8,128)S(1)}, u32[]{:S(2)}, u32[]{:S(2)}) async-start(f32[32,8,256]{2,1,0:T(8,128)} %bitcast.60), calls=%async_computation.14 | async-start | bytes 524288 | tf_op jit(solution)/shard_map/all_to_all | solution.py:101
  422.1 71.7 %reduce-scatter.17.cloned.1.call-start = ((), (), s32[]{:S(2)}) async-start(), calls=%async_computation.23 | async-start | bytes 655360 | tf_op jit(solution)/shard_map/reduce_scatter | solution.py:98
  469.6 31.1 %collective-permute-start.10 = (f32[256,256]{1,0:T(8,128)S(1)}, f32[256,256]{1,0:T(8,128)S(1)}, u32[]{:S(2)}, u32[]{:S(2)}) collective-permute-start(f32[256,256]{1,0:T(8,128)S(1)} %get-tuple-element.21), channel_id=1, source_target_pairs={{0,1},{1,2},{2,3},{3,4},{4,5},{5,6},{6,7},{7,8},{8,9},{9,10},{10,1... | collective-permute-start | bytes 786440 | tf_op jit(solution)/shard_map/ppermute | solution.py:15
  471.4 29.3 %collective-permute-start.11 = (f32[256,256]{1,0:T(8,128)S(1)}, f32[256,256]{1,0:T(8,128)S(1)}, u32[]{:S(2)}, u32[]{:S(2)}) collective-permute-start(f32[256,256]{1,0:T(8,128)S(1)} %get-tuple-element.22), channel_id=1, source_target_pairs={{1,0},{2,1},{3,2},{4,3},{5,4},{6,5},{7,6},{8,7},{9,8},{10,9},{11,1... | collective-permute-start | bytes 786440 | tf_op jit(solution)/shard_map/ppermute | solution.py:18
  496.5 15.7 %all-to-all-start.11 = ((f32[32,8,256]{2,1,0:T(8,128)}), f32[32,8,256]{2,1,0:T(8,128)S(1)}, u32[]{:S(2)}, u32[]{:S(2)}) async-start(f32[32,8,256]{2,1,0:T(8,128)} %bitcast.71), calls=%async_computation.17 | async-start | bytes 524288 | tf_op jit(solution)/shard_map/all_to_all | solution.py:101
Sparse Core Ops, SparseCore 0:
  60.1 19.7 reduce-scatter.6
  131.9 24.8 reduce-scatter.8
  210.6 24.8 reduce-scatter.10
  311.6 24.8 reduce-scatter.12
  389.9 24.8 reduce-scatter.14
  468.7 25.0 reduce-scatter.16
